TPU v7x, 32 devices: a whole 2x2x4 slice. The times are simulated.
32 devices in a mesh: utt: 4 (over y, core), clu: 8 (over z, x).
Axes of the slice: x: 2, y: 2, z: 4, core: 2. Of those that a mesh axis runs over, the one named last changes fastest.
Arguments:
- features: bfloat16 [65536, 1280], P(('utt', 'clu')), may hold values from -1.75 to 1.75
- centroids: bfloat16 [1024, 1280], P('clu'), may hold values from -2 to 2
- route: int32 [32, 32], P(('utt', 'clu')), may hold values from 0 to 31, each once within a row
Outputs:
- trainer_labels: int32 [32, 32, 64], P(('utt', 'clu'))
- trainer_distance: float32 [32, 32, 64], P(('utt', 'clu'))
Inputs may be any that keep to these rules, and one draw needn't show every extreme that they name: Each row of route names every trainer device exactly once.
All inputs are finite; a program needn't handle non-finite values.
Results may differ from a plain program's by a relative error of at most 0.0003.
Values may be sent and summed in bfloat16 or wider, within the bound.
A program may use at most 64 MiB of HBM per device.

v0:
```python
import jax
import jax.numpy as jnp
from jax import lax
from jax.sharding import PartitionSpec as P


def per_device(features, centroids, route):
    rows = features.shape[0]
    width = features.shape[1]
    block = 512
    count = rows // block
    feat_blocks = features.reshape(count, block, width)
    frame_sq = jnp.sum(jnp.square(features.astype(jnp.float32)), axis=1).reshape(count, block)
    piece = lax.all_gather(centroids, "clu", axis=0, tiled=True)
    best_dist = jnp.full((count, block), jnp.inf, jnp.float32)
    best_index = jnp.zeros((count, block), jnp.int32)
    cent_sq = jnp.sum(jnp.square(piece.astype(jnp.float32)), axis=1)

    def one_block(items):
        feats, squares, held_dist, held_index = items
        inner = jnp.dot(feats, piece.T, preferred_element_type=jnp.float32)
        dist = (squares[:, None] - 2.0 * inner + cent_sq[None, :]) / width
        found = jnp.min(dist, axis=1)
        where = jnp.argmin(dist, axis=1)
        better = (found < held_dist) | (found == held_dist) & (where < held_index)
        return (jnp.where(better, found, held_dist), jnp.where(better, where, held_index))

    least, labels = lax.map(one_block, (feat_blocks, frame_sq, best_dist, best_index))
    n_utt = lax.axis_size("utt")
    n_clu = lax.axis_size("clu")
    devices = n_utt * n_clu
    per_block = rows // devices
    labels = labels.reshape(devices, per_block)
    least = least.reshape(devices, per_block)
    inverse = jnp.argsort(route[0])
    sent_labels = labels[inverse]
    sent_least = least[inverse]
    got_labels, got_least = (
        lax.all_to_all(sent_labels, ("utt", "clu"), split_axis=0, concat_axis=0, tiled=True),
        lax.all_to_all(sent_least, ("utt", "clu"), split_axis=0, concat_axis=0, tiled=True),
    )
    return (got_labels.reshape(1, devices, per_block), got_least.reshape(1, devices, per_block))


def solution(mesh):
    placed = (P(("utt", "clu"), None), P("clu", None), P(("utt", "clu"), None))
    return jax.shard_map(
        per_device,
        mesh=mesh,
        in_specs=placed,
        out_specs=(P(("utt", "clu"), None, None), P(("utt", "clu"), None, None)),
        check_vma=False,
    )
```

profile of v0, /device:TPU:0, one launch (start us, length us, event | category | flops | bytes accessed | tf_op | source)
XLA Modules:
  0.0 114.2 jit_solution(7918610181267504825)
XLA Ops:
  7.2 0.0 all-gather.2.cloned.1.call-start
  7.2 0.7 all-gather.2.cloned.1.call-update
  7.9 0.0 copy-start.1
  7.9 3.6 %multiply_reduce_fusion = f32[2048]{0:T(1024)S(1)} fusion(bf16[2048,1280]{1,0:T(8,128)(2,1)} %param.5), kind=kLoop, calls=%fused_computation.10 | loop fusion | flops 7862272 | bytes 5251072 | tf_op jit(solution)/shard_map/reduce_sum | solution.py:13
  11.5 0.0 copy-done.1
  11.5 1.6 %sort.17 = (s32[32]{0:T(128)}, s32[32]{0:T(128)S(1)}) sort(s32[32]{0:T(128)S(1)} %bitcast.33, s32[32]{0:T(128)S(1)} %iota.11), dimensions={0}, to_apply=%region_5.6 | sort | flops 160 | bytes 512 | tf_op jit(solution)/shard_map/jit(argsort)/sort | solution.py:35
  13.2 54.2 %all-gather.2.cloned.1.call-done = bf16[1024,1280]{1,0:T(8,128)(2,1)} async-done(((bf16[128,1280]{1,0:T(8,128)(2,1)}), bf16[1024,1280]{1,0:T(8,128)(2,1)}) %all-gather.2.cloned.1.call-update) | async-done | bytes 2621456 | tf_op jit(solution)/shard_map/all_gather | solution.py:14
  67.3 2.5 %multiply_reduce_fusion.1 = f32[1024]{0:T(1024)S(1)} fusion(bf16[1024,1280]{1,0:T(8,128)(2,1)} %all-gather.2.cloned.1.call-done), kind=kLoop, calls=%fused_computation.11 | loop fusion | flops 3931136 | bytes 2625536 | tf_op jit(solution)/shard_map/reduce_sum | solution.py:17
  69.8 0.1 copy-done
  69.9 15.1 %while.12 = (s32[]{:T(128)}, f32[4,512]{1,0:T(4,128)S(1)}, s32[4,512]{1,0:T(4,128)S(1)}, f32[4,512]{1,0:T(4,128)S(1)}, bf16[4,512,1280]{2,1,0:T(8,128)(2,1)}, /*...) while((s32[]{:T(128)}, f32[4,512]{1,0:T(4,128)S(1)}, ...), condition=%wide.region_4.5_spmd, body=%wide.region_2.4_spmd.sunk | while | flops 1348994560 | bytes 3967593 | solution.py:28
  69.9 3.6 %iota_reduce_fusion.2 = (f32[512]{0:T(512)S(1)}, s32[512]{0:T(512)S(1)}) fusion(bf16[1024,1280]{1,0:T(8,128)(2,1)S(1)} %get-tuple-element.131, bf16[4,512,1280]{2,1,0:T(8,128)(2,1)} %get-tuple-element.130, s32[]{:T(128)} %get-tuple-element.117, f32[1024]{0:T(1024)S(1)} %get-tuple-element.132, f32[512]{0:T(512)S(1)} %bitcast.32), kind=kOutput, calls=%fused_computation.2.clone.1 | convolution fusion | flops 1348988416 | bytes 3942912 | tf_op jit(solution)/shard_map/while/body/eval_jaxpr/dot_general | solution.py:21
  73.5 0.1 dynamic_update_slice.11
  73.6 0.1 dynamic_update_slice.10
  73.6 3.6 %iota_reduce_fusion.2 = (f32[512]{0:T(512)S(1)}, s32[512]{0:T(512)S(1)}) fusion(bf16[1024,1280]{1,0:T(8,128)(2,1)S(1)} %get-tuple-element.131, bf16[4,512,1280]{2,1,0:T(8,128)(2,1)} %get-tuple-element.130, s32[]{:T(128)} %get-tuple-element.117, f32[1024]{0:T(1024)S(1)} %get-tuple-element.132, f32[512]{0:T(512)S(1)} %bitcast.32), kind=kOutput, calls=%fused_computation.2.clone.1 | convolution fusion | flops 1348988416 | bytes 3942912 | tf_op jit(solution)/shard_map/while/body/eval_jaxpr/dot_general | solution.py:21
  77.3 0.1 dynamic_update_slice.11
  77.3 0.1 dynamic_update_slice.10
  77.4 3.6 %iota_reduce_fusion.2 = (f32[512]{0:T(512)S(1)}, s32[512]{0:T(512)S(1)}) fusion(bf16[1024,1280]{1,0:T(8,128)(2,1)S(1)} %get-tuple-element.131, bf16[4,512,1280]{2,1,0:T(8,128)(2,1)} %get-tuple-element.130, s32[]{:T(128)} %get-tuple-element.117, f32[1024]{0:T(1024)S(1)} %get-tuple-element.132, f32[512]{0:T(512)S(1)} %bitcast.32), kind=kOutput, calls=%fused_computation.2.clone.1 | convolution fusion | flops 1348988416 | bytes 3942912 | tf_op jit(solution)/shard_map/while/body/eval_jaxpr/dot_general | solution.py:21
  81.1 0.1 dynamic_update_slice.11
  81.1 0.1 dynamic_update_slice.10
  81.2 3.6 %iota_reduce_fusion.2 = (f32[512]{0:T(512)S(1)}, s32[512]{0:T(512)S(1)}) fusion(bf16[1024,1280]{1,0:T(8,128)(2,1)S(1)} %get-tuple-element.131, bf16[4,512,1280]{2,1,0:T(8,128)(2,1)} %get-tuple-element.130, s32[]{:T(128)} %get-tuple-element.117, f32[1024]{0:T(1024)S(1)} %get-tuple-element.132, f32[512]{0:T(512)S(1)} %bitcast.32), kind=kOutput, calls=%fused_computation.2.clone.1 | convolution fusion | flops 1348988416 | bytes 3942912 | tf_op jit(solution)/shard_map/while/body/eval_jaxpr/dot_general | solution.py:21
  84.8 0.1 dynamic_update_slice.11
  84.9 0.1 dynamic_update_slice.10
  85.0 0.1 reshape.33
  85.1 1.2 %gather_fusion = s32[32,64]{1,0:T(8,128)} fusion(s32[32,64]{1,0:T(8,128)S(1)} %reshape.33, s32[1024]{0:T(1024)S(1)} %pad_clamp_fusion), kind=kCustom, calls=%fused_computation | custom fusion | bytes 16512 | tf_op jit(solution)/shard_map/gather | solution.py:36
  86.2 3.2 %all-to-all-start = ((s32[32,1,64]{2,1,0:T(1,128)}), s32[32,1,64]{2,1,0:T(1,128)S(1)}, u32[]{:S(2)}, u32[]{:S(2)}) async-start(s32[32,1,64]{2,1,0:T(1,128)} %bitcast.7), calls=%async_computation | async-start | bytes 32768 | tf_op jit(solution)/shard_map/all_to_all | solution.py:39
  89.4 0.1 reshape.35
  89.5 1.2 %gather_fusion.1 = f32[32,64]{1,0:T(8,128)} fusion(f32[32,64]{1,0:T(8,128)S(1)} %reshape.35, s32[1024]{0:T(1024)S(1)} %pad_clamp_fusion), kind=kCustom, calls=%fused_computation.1 | custom fusion | bytes 16512 | tf_op jit(solution)/shard_map/gather | solution.py:37
  90.7 5.8 %all-to-all-done = s32[32,1,64]{2,1,0:T(1,128)S(1)} async-done(((s32[32,1,64]{2,1,0:T(1,128)}), s32[32,1,64]{2,1,0:T(1,128)S(1)}, u32[]{:S(2)}, u32[]{:S(2)}) %all-to-all-start) | async-done | bytes 8224 | tf_op jit(solution)/shard_map/all_to_all | solution.py:39
  96.5 2.5 %all-to-all-start.1 = ((f32[32,1,64]{2,1,0:T(1,128)}), f32[32,1,64]{2,1,0:T(1,128)S(1)}, u32[]{:S(2)}, u32[]{:S(2)}) async-start(f32[32,1,64]{2,1,0:T(1,128)} %bitcast.10), calls=%async_computation.1 | async-start | bytes 32768 | tf_op jit(solution)/shard_map/all_to_all | solution.py:40
  99.0 7.1 %all-to-all-done.1 = f32[32,1,64]{2,1,0:T(1,128)S(1)} async-done(((f32[32,1,64]{2,1,0:T(1,128)}), f32[32,1,64]{2,1,0:T(1,128)S(1)}, u32[]{:S(2)}, u32[]{:S(2)}) %all-to-all-start.1) | async-done | bytes 8224 | tf_op jit(solution)/shard_map/all_to_all | solution.py:40
  106.1 0.6 copy.20
  106.7 0.6 copy.21
  (19 shorter events, 0.1 us)
Async XLA Ops:
  7.2 60.2 %all-gather.2.cloned.1.call-start = ((), (), s32[]{:S(2)}) async-start(), calls=%async_computation.2 | async-start | bytes 2949120 | tf_op jit(solution)/shard_map/all_gather | solution.py:14
  7.9 3.6 %copy-start.1 = (s32[1,32]{1,0:T(1,128)S(1)}, s32[1,32]{1,0:T(1,128)}, u32[]{:S(2)}) copy-start(s32[1,32]{1,0:T(1,128)} %param.7) | copy-start | bytes 388
  67.3 2.5 %copy-start = (bf16[1024,1280]{1,0:T(8,128)(2,1)S(1)}, bf16[1024,1280]{1,0:T(8,128)(2,1)}, u32[]{:S(2)}) copy-start(bf16[1024,1280]{1,0:T(8,128)(2,1)} %all-gather.2.cloned.1.call-done) | copy-start | bytes 7864324
  86.2 10.3 %all-to-all-start = ((s32[32,1,64]{2,1,0:T(1,128)}), s32[32,1,64]{2,1,0:T(1,128)S(1)}, u32[]{:S(2)}, u32[]{:S(2)}) async-start(s32[32,1,64]{2,1,0:T(1,128)} %bitcast.7), calls=%async_computation | async-start | bytes 32768 | tf_op jit(solution)/shard_map/all_to_all | solution.py:39
  96.5 9.6 %all-to-all-start.1 = ((f32[32,1,64]{2,1,0:T(1,128)}), f32[32,1,64]{2,1,0:T(1,128)S(1)}, u32[]{:S(2)}, u32[]{:S(2)}) async-start(f32[32,1,64]{2,1,0:T(1,128)} %bitcast.10), calls=%async_computation.1 | async-start | bytes 32768 | tf_op jit(solution)/shard_map/all_to_all | solution.py:40
Sparse Core Ops, SparseCore 0:
  10.2 57.1 all-gather.1
where the time goes:
time: 114 us
  waiting for transfers between devices  67.7 us (59%)
  matrix products  14.5 us (13%)
  between operations  14.1 us (12%)
  other arithmetic  7.72 us (7%)
  starting transfers between devices  5.77 us (5%)
  local copies, waits for them, and re-layouts  4.21 us (4%)
    all_gather x1, waiting for transfers between devices, per_device(): piece = lax.all_gather(centroids, 'clu', axis=0, tiled=True)  54.2 us
    dot_general x4, matrix products, one_block(): inner = jnp.dot(feats, piece.T, preferred_element_type=jnp.float32)  14.5 us
    all_to_all x1, waiting for transfers between devices, per_device(): lax.all_to_all(sent_least, ('utt', 'clu'), split_axis=0, concat_axis=0, t...  7.07 us
    all_to_all x1, waiting for transfers between devices, per_device(): lax.all_to_all(sent_labels, ('utt', 'clu'), split_axis=0, concat_axis=0,...  5.82 us
    reduce_sum x1, other arithmetic, per_device(): jnp.sum(jnp.square(features.astype(jnp.float32)), axis=1)  3.58 us
    all_to_all x1, starting transfers between devices, per_device(): lax.all_to_all(sent_labels, ('utt', 'clu'), split_axis=0, concat_axis=0,...  3.19 us
    all_to_all x1, starting transfers between devices, per_device(): lax.all_to_all(sent_least, ('utt', 'clu'), split_axis=0, concat_axis=0, t...  2.54 us
    reduce_sum x1, other arithmetic, per_device(): cent_sq = jnp.sum(jnp.square(piece.astype(jnp.float32)), axis=1)  2.47 us
  transfers between devices with their start and end apart: 3, of which 3 were waited for; matrix products, arithmetic and copies ran while one was open for 6% of the time, Pallas kernels for 0%

commit v1 on v0

v1 whole, which is shorter than its diff:
```python
import functools

import jax
import jax.numpy as jnp
from jax import lax
from jax.experimental import pallas as pl
from jax.experimental.pallas import tpu as pltpu
from jax.sharding import PartitionSpec as P

LANES = 128


def lane_sums(rows):
    wide = rows.astype(jnp.float32)
    wide = wide * wide
    part = wide[:, :LANES]
    for j in range(1, rows.shape[1] // LANES):
        part = part + wide[:, j * LANES:(j + 1) * LANES]
    return jnp.sum(part.T, axis=0, keepdims=True)


def kernel(n_utt, n_clu, n_x, feat_hbm, cent_hbm, route_ref, lab_out, dist_out,
           feat, cent, val, idx, fsq, csq, res, sent, got,
           feat_sem, own_sem, z_send, z_recv, x_send, x_recv, c_send, c_recv, a_send, a_recv):
    n_z = n_clu // n_x
    devices = n_utt * n_clu
    utt, clu = lax.axis_index("utt"), lax.axis_index("clu")
    me = utt * n_clu + clu
    half, x, z = utt % 2, clu % n_x, clu // n_x
    frames, width = feat.shape
    tile = frames // feat_sem.shape[0]
    per_block = frames // devices

    def xor(a, b):
        out, bit = a, 1
        while bit <= b:
            if b & bit:
                out = out + bit * (1 - 2 * ((a // bit) % 2))
            bit *= 2
        return out

    def slot(r, s):
        return xor(z, r) * n_x + xor(x, s)

    partner = xor(utt, 1)
    own = pltpu.make_async_copy(cent_hbm, cent.at[clu], own_sem)
    own.start()

    def feat_copy(t):
        span = pl.ds(t * tile, tile)
        return pltpu.make_async_copy(feat_hbm.at[span], feat.at[span], feat_sem.at[t])

    for t in range(frames // tile):
        feat_copy(t).start()

    barrier = pltpu.get_barrier_semaphore()

    def greet(j, carry):
        other = lax.rem(me + j, devices)
        pl.semaphore_signal(barrier, inc=1, device_id=(other // n_clu, other % n_clu),
                            device_id_type=pl.DeviceIdType.MESH)
        return carry

    lax.fori_loop(1, devices, greet, 0)

    def remote(piece, send, recv, u, w):
        return pltpu.make_async_remote_copy(src_ref=piece, dst_ref=piece, send_sem=send, recv_sem=recv,
                                            device_id=(u, w), device_id_type=pl.DeviceIdType.MESH)

    def z_copy(r, incoming=False):
        piece = cent.at[slot(r, 0) if incoming else clu, half]
        return remote(piece, z_send.at[r], z_recv.at[r], utt, slot(r, 0))

    def x_copy(r, s, incoming=False):
        piece = cent.at[slot(r, s if incoming else 0), half]
        return remote(piece, x_send.at[r, s], x_recv.at[r, s], utt, slot(0, s))

    def c_copy(r, s, incoming=False):
        piece = cent.at[slot(r, s), (1 - half) if incoming else half]
        return remote(piece, c_send.at[r, s], c_recv.at[r, s], partner, clu)

    own.wait()
    pl.semaphore_wait(barrier, devices - 1)
    for s in range(1, n_x):
        x_copy(0, s).start()
    for r in range(1, n_z):
        z_copy(r).start()

    def relay_z(r):
        z_copy(r, True).wait_recv()
        for s in range(1, n_x):
            x_copy(r, s).start()
        c_copy(r, 0).start()

    def relay_x(r):
        for s in range(1, n_x):
            x_copy(r, s, True).wait_recv()
            c_copy(r, s).start()

    def block(w):
        return cent[w].reshape(-1, width)

    def compute(chunks, first=False):
        for i, w in enumerate(chunks):
            csq[0:1, i * LANES:(i + 1) * LANES] = lane_sums(block(w))
        n = len(chunks)
        step = 512

        @pl.loop(0, frames // step)
        def _(t):
            span = pl.ds(pl.multiple_of(t * step, step), step)
            rhs = block(chunks[0]) if n == 1 else jnp.concatenate([block(w) for w in chunks], axis=0)
            inner = lax.dot_general(feat[span, :], rhs, (((1,), (1,)), ((), ())),
                                    preferred_element_type=jnp.float32)
            d = csq[0:1, :n * LANES] - 2.0 * inner
            if first:
                v, k = d[:, :LANES], jnp.full((step, LANES), chunks[0], jnp.int32)
            else:
                v, k = val[span, :], idx[span, :]
            for i in range(1 if first else 0, n):
                new = d[:, i * LANES:(i + 1) * LANES]
                better = (new < v) | ((new == v) & (chunks[i] < k))
                v = jnp.where(better, new, v)
                k = jnp.where(better, chunks[i], k)
            val[span, :] = v
            idx[span, :] = k

    for t in range(frames // tile):
        feat_copy(t).wait()
    compute([slot(0, 0)], first=True)
    relay_x(0)
    relay_z(1)

    @pl.loop(0, frames // LANES)
    def _(t):
        fsq[t] = lane_sums(feat[pl.ds(pl.multiple_of(t * LANES, LANES), LANES), :])

    for r in range(n_z):
        pairs = [(r, s) for s in range(1, n_x)] + ([(r + 1, 0)] if r + 1 < n_z else [])
        for pair in pairs:
            c_copy(*pair, True).wait_recv()
        compute([slot(*pair) for pair in pairs])
        if r + 1 < n_z:
            relay_x(r + 1)
        if r + 2 < n_z:
            relay_z(r + 2)

    lane = lax.broadcasted_iota(jnp.int32, (1, LANES), 1)
    blocks = LANES // per_block

    @pl.loop(0, frames // LANES)
    def _(t):
        span = pl.ds(pl.multiple_of(t * LANES, LANES), LANES)
        v = val[span, :].T
        k = (idx[span, :] * LANES + lax.broadcasted_iota(jnp.int32, (LANES, LANES), 1)).astype(jnp.float32).T
        least = jnp.min(v, axis=0, keepdims=True)
        label = jnp.min(jnp.where(v == least, k, float(n_clu * LANES)), axis=0, keepdims=True)
        dist = (fsq[t] + least) / width
        for j in range(blocks):
            a = label if j == 0 else pltpu.roll(label, LANES - per_block * j, 1)
            shift = (per_block - per_block * j) % LANES
            b = dist if shift == 0 else pltpu.roll(dist, shift, 1)
            res[pl.ds(t * blocks + j, 1), :] = jnp.where(lane < per_block, a, b)

    pick = (route_ref[...] == lax.broadcasted_iota(jnp.int32, (devices, devices), 0)).astype(jnp.float32)
    sent[...] = jnp.dot(pick, res[...], preferred_element_type=jnp.float32,
                        precision=lax.Precision.HIGHEST).reshape(sent.shape)

    def out_copy(j, incoming):
        dst = lax.rem(me + j, devices)
        src = lax.rem(me + devices - j, devices)
        return pltpu.make_async_remote_copy(
            src_ref=sent.at[dst], dst_ref=got.at[src if incoming else me],
            send_sem=a_send.at[j], recv_sem=a_recv.at[j],
            device_id=(dst // n_clu, dst % n_clu), device_id_type=pl.DeviceIdType.MESH)

    def send(j, carry):
        out_copy(j, False).start()
        return carry

    lax.fori_loop(1, devices, send, 0)
    got[me] = sent[me]
    for r in range(n_z):
        for s in range(n_x):
            if s:
                x_copy(r, s).wait_send()
            elif r:
                z_copy(r).wait_send()
            if r or s:
                c_copy(r, s).wait_send()

    def receive(j, carry):
        out_copy(j, True).wait_recv()
        return carry

    lax.fori_loop(1, devices, receive, 0)
    table = got[...].reshape(devices, LANES)
    lab_out[...] = table[:, :per_block].astype(jnp.int32)
    dist_out[...] = table[:, per_block:2 * per_block]

    def sent_off(j, carry):
        out_copy(j, False).wait_send()
        return carry

    lax.fori_loop(1, devices, sent_off, 0)


def per_device(n_utt, n_clu, features, centroids, route):
    frames, width = features.shape
    rows = centroids.shape[0]
    devices = n_utt * n_clu
    n_x = 1
    while n_x * n_x * 4 <= n_clu:
        n_x *= 2
    n_z = n_clu // n_x
    per_block = frames // devices
    tiles = 4
    dma = pltpu.SemaphoreType.DMA
    cent = centroids.reshape(2, rows // 2, width)
    labels, least = pl.pallas_call(
        functools.partial(kernel, n_utt, n_clu, n_x),
        out_shape=(jax.ShapeDtypeStruct((devices, per_block), jnp.int32),
                   jax.ShapeDtypeStruct((devices, per_block), jnp.float32)),
        in_specs=[pl.BlockSpec(memory_space=pl.ANY), pl.BlockSpec(memory_space=pl.ANY),
                  pl.BlockSpec(memory_space=pltpu.VMEM)],
        out_specs=(pl.BlockSpec(memory_space=pltpu.VMEM), pl.BlockSpec(memory_space=pltpu.VMEM)),
        scratch_shapes=[
            pltpu.VMEM((frames, width), features.dtype),
            pltpu.VMEM((n_clu, 2, rows // 2, width), centroids.dtype),
            pltpu.VMEM((frames, LANES), jnp.float32),
            pltpu.VMEM((frames, LANES), jnp.int32),
            pltpu.VMEM((frames // LANES, 1, LANES), jnp.float32),
            pltpu.VMEM((8, n_x * LANES), jnp.float32),
            pltpu.VMEM((devices, LANES), jnp.float32),
            pltpu.VMEM((devices, 1, LANES), jnp.float32),
            pltpu.VMEM((devices, 1, LANES), jnp.float32),
            dma((tiles,)), dma(()),
            dma((n_z,)), dma((n_z,)),
            dma((n_z, n_x)), dma((n_z, n_x)),
            dma((n_z, n_x)), dma((n_z, n_x)),
            dma((devices,)), dma((devices,)),
        ],
        compiler_params=pltpu.CompilerParams(
            collective_id=0, has_side_effects=True, vmem_limit_bytes=60 * 1024 * 1024),
        name="nearest",
    )(features, cent, route)
    return labels.reshape(1, devices, per_block), least.reshape(1, devices, per_block)


def solution(mesh):
    placed = (P(("utt", "clu"), None), P("clu", None), P(("utt", "clu"), None))
    return jax.shard_map(
        functools.partial(per_device, mesh.shape["utt"], mesh.shape["clu"]),
        mesh=mesh,
        in_specs=placed,
        out_specs=(P(("utt", "clu"), None, None), P(("utt", "clu"), None, None)),
        check_vma=False,
    )
```

time: 114 us -> 46.2 us (0.41)
  waiting for transfers between devices: 67.7 us -> 0 us
  Pallas kernels: 0 us -> 42.6 us
  matrix products: 14.5 us -> 0 us
  between operations: 14.1 us -> 0.64 us
  other arithmetic: 7.72 us -> 0 us
  starting transfers between devices: 5.77 us -> 0 us
  local copies, waits for them, and re-layouts: 4.21 us -> 2.65 us
    all_gather x1 -> x0, waiting for transfers between devices: 54.2 us -> none  [per_device(): piece = lax.all_gather(centroids, 'clu', axis=0, tiled=True)]
    pallas_call x0 -> x1, Pallas kernels: none -> 42.6 us  [per_device(): pl.pallas_call(functools.partial(kernel, n_utt, n_clu, n_x), out_shape=(j...]
    dot_general x4 -> x0, matrix products: 14.5 us -> none  [one_block(): inner = jnp.dot(feats, piece.T, preferred_element_type=jnp.float32)]
    all_to_all x2 -> x0, waiting for transfers between devices: 12.9 us -> none  [the longest x1 7.07 us: per_device(): lax.all_to_all(sent_least, ('utt', 'clu'), split_axis=0, concat_axis=0, t...]
    reduce_sum x2 -> x0, other arithmetic: 6.05 us -> none  [the longest x1 3.58 us: per_device(): jnp.sum(jnp.square(features.astype(jnp.float32)), axis=1)]
    all_to_all x2 -> x0, starting transfers between devices: 5.73 us -> none  [the longest x1 3.19 us: per_device(): lax.all_to_all(sent_labels, ('utt', 'clu'), split_axis=0, concat_axis=0,...]
    gather x2 -> x0, local copies, waits for them, and re-layouts: 2.33 us -> none  [the longest x1 1.17 us: per_device(): sent_labels = labels[inverse]]
    sort x1 -> x0, other arithmetic: 1.61 us -> none  [per_device(): inverse = jnp.argsort(route[0])]
  transfers between devices with their start and end apart: 3 -> 0, of which waited for: 3 -> 0; matrix products, arithmetic and copies ran while one was open for 6% -> 0% of each run, Pallas kernels for 0% -> 0%
where the time goes in v1:
time: 46.2 us; the launch traced here: 45.9 us
  Pallas kernels  42.6 us (92%)
  local copies, waits for them, and re-layouts  2.65 us (6%)
  between operations  0.64 us (1%)
    pallas_call x1, Pallas kernels, per_device(): pl.pallas_call(functools.partial(kernel, n_utt, n_clu, n_x), out_shape=(j...  42.6 us
    unnamed x2, local copies, waits for them, and re-layouts  2.65 us

profile of v1, /device:TPU:0, one launch (start us, length us, event | category | flops | bytes accessed | tf_op | source)
XLA Modules:
  0.0 45.9 jit_solution(3284626266822941348)
XLA Ops:
  0.6 42.6 %nearest.1 = (s32[32,64]{1,0:T(8,128)}, f32[32,64]{1,0:T(8,128)}) custom-call(bf16[2048,1280]{1,0:T(8,128)(2,1)} %feat_hbm.1, bf16[2,64,1280]{2,1,0:T(8,128)(2,1)} %bitcast.3, s32[1,32]{1,0:T(1,128)} %route_ref.1), custom_call_target="tpu_custom_call" | custom-call | tf_op jit(solution)/shard_map/nearest/pallas_call | solution.py:220
  43.2 1.3 %copy.7 = s32[1,32,64]{2,1,0:T(8,128)} copy(s32[1,32,64]{2,1,0:T(8,128)} %bitcast.5) | data formatting | bytes 16384
  44.5 1.3 %copy.8 = f32[1,32,64]{2,1,0:T(8,128)} copy(f32[1,32,64]{2,1,0:T(8,128)} %bitcast.4) | data formatting | bytes 16384

commit v2 on v1

v2 whole, which is shorter than its diff:
```python
import functools

import jax
import jax.numpy as jnp
from jax import lax
from jax.experimental import pallas as pl
from jax.experimental.pallas import tpu as pltpu
from jax.sharding import PartitionSpec as P

LANES = 128


def lane_sums(rows):
    wide = rows.astype(jnp.float32)
    wide = wide * wide
    part = wide[:, :LANES]
    for j in range(1, rows.shape[1] // LANES):
        part = part + wide[:, j * LANES:(j + 1) * LANES]
    return jnp.sum(part.T, axis=0, keepdims=True)


def kernel(n_utt, n_clu, n_x, feat_hbm, cent_hbm, route_ref, out,
           feat, cent, val, idx, fsq, csq, res, sent, got,
           feat_sem, own_sem, z_send, z_recv, x_send, x_recv, y_send, y_recv, c_send, c_recv, a_send, a_recv):
    n_z = n_clu // n_x
    devices = n_utt * n_clu
    utt, clu = lax.axis_index("utt"), lax.axis_index("clu")
    me = utt * n_clu + clu
    n_y = n_utt // 2
    half, y, x, z = utt % 2, utt // 2, clu % n_x, clu // n_x
    frames, width = feat.shape
    tile = frames // feat_sem.shape[0]
    per_block = frames // devices

    def xor(a, b):
        out, bit = a, 1
        while bit <= b:
            if b & bit:
                out = out + bit * (1 - 2 * ((a // bit) % 2))
            bit *= 2
        return out

    def slot(r, s):
        return xor(z, r) * n_x + xor(x, s)

    partner = xor(utt, 1)
    own = pltpu.make_async_copy(cent_hbm, cent.at[clu], own_sem)
    own.start()

    def feat_copy(t):
        span = pl.ds(t * tile, tile)
        return pltpu.make_async_copy(feat_hbm.at[span], feat.at[span], feat_sem.at[t])

    for t in range(frames // tile):
        feat_copy(t).start()

    barrier = pltpu.get_barrier_semaphore()
    peers = ([(utt, slot(r, 0)) for r in range(1, n_z)] + [(utt, slot(0, s)) for s in range(1, n_x)]
             + [(xor(utt, 2 * t), clu) for t in range(1, n_y)] + [(partner, clu)])
    for peer in peers:
        pl.semaphore_signal(barrier, inc=1, device_id=peer, device_id_type=pl.DeviceIdType.MESH)

    def remote(piece, send, recv, u, w):
        return pltpu.make_async_remote_copy(src_ref=piece, dst_ref=piece, send_sem=send, recv_sem=recv,
                                            device_id=(u, w), device_id_type=pl.DeviceIdType.MESH)

    def z_copy(r, incoming=False):
        piece = cent.at[slot(r, 0) if incoming else clu, half, y]
        return remote(piece, z_send.at[r], z_recv.at[r], utt, slot(r, 0))

    def x_copy(r, s, incoming=False):
        piece = cent.at[slot(r, s if incoming else 0), half]
        return remote(piece.at[y] if r else piece, x_send.at[r, s], x_recv.at[r, s], utt, slot(0, s))

    def y_copy(r, s, t, incoming=False):
        piece = cent.at[slot(r, s), half, xor(y, t) if incoming else y]
        return remote(piece, y_send.at[r, s, t], y_recv.at[r, s, t], xor(utt, 2 * t), clu)

    def c_copy(r, s, incoming=False):
        piece = cent.at[slot(r, s), (1 - half) if incoming else half]
        return remote(piece, c_send.at[r, s], c_recv.at[r, s], partner, clu)

    own.wait()
    pl.semaphore_wait(barrier, len(peers))
    for s in range(1, n_x):
        x_copy(0, s).start()
    for r in range(1, n_z):
        z_copy(r).start()

    def relay_z(r):
        if r < n_z:
            z_copy(r, True).wait_recv()
            for s in range(1, n_x):
                x_copy(r, s).start()
            for t in range(1, n_y):
                y_copy(r, 0, t).start()

    def relay_x(r):
        if r < n_z:
            for s in range(1, n_x):
                x_copy(r, s, True).wait_recv()
                if r:
                    for t in range(1, n_y):
                        y_copy(r, s, t).start()
                else:
                    c_copy(r, s).start()

    def relay_y(r, s):
        if 0 < r < n_z:
            for t in range(1, n_y):
                y_copy(r, s, t, True).wait_recv()
            c_copy(r, s).start()

    def block(w):
        return cent[w].reshape(-1, width)

    lane = lax.broadcasted_iota(jnp.int32, (1, LANES), 1)
    blocks = LANES // per_block
    step = 512

    def finish(t, v, k):
        v = v.T
        k = (k * LANES + lane).astype(jnp.float32).T
        least = jnp.min(v, axis=0, keepdims=True)
        label = jnp.min(jnp.where(v == least, k, float(n_clu * LANES)), axis=0, keepdims=True)
        dist = (fsq[t] + least) / width
        for j in range(blocks):
            a = label if j == 0 else pltpu.roll(label, LANES - per_block * j, 1)
            shift = (per_block - per_block * j) % LANES
            b = dist if shift == 0 else pltpu.roll(dist, shift, 1)
            res[pl.ds(t * blocks + j, 1), :] = jnp.where(lane < per_block, a, b)

    def compute(chunks, start, stop, first=False, last=False):
        n = len(chunks)
        if start == 0:
            for i, w in enumerate(chunks):
                csq[0:1, i * LANES:(i + 1) * LANES] = lane_sums(block(w))

        @pl.loop(start, stop)
        def _(t):
            span = pl.ds(pl.multiple_of(t * step, step), step)
            rhs = block(chunks[0]) if n == 1 else jnp.concatenate([block(w) for w in chunks], axis=0)
            inner = lax.dot_general(feat[span, :], rhs, (((1,), (1,)), ((), ())),
                                    preferred_element_type=jnp.float32)
            d = csq[0:1, :n * LANES] - 2.0 * inner
            if first:
                v, k = d[:, :LANES], jnp.full((step, LANES), chunks[0], jnp.int32)
            else:
                v, k = val[span, :], idx[span, :]
            for i in range(1 if first else 0, n):
                new = d[:, i * LANES:(i + 1) * LANES]
                better = (new < v) | ((new == v) & (chunks[i] < k))
                v = jnp.where(better, new, v)
                k = jnp.where(better, chunks[i], k)
            if last:
                for i in range(step // LANES):
                    part = slice(i * LANES, (i + 1) * LANES)
                    finish(t * (step // LANES) + i, v[part], k[part])
            else:
                val[span, :] = v
                idx[span, :] = k

    def squares(start, stop):
        @pl.loop(start, stop)
        def _(t):
            fsq[t] = lane_sums(feat[pl.ds(pl.multiple_of(t * LANES, LANES), LANES), :])

    for t in range(frames // tile):
        feat_copy(t).wait()
    steps, tiles = frames // step, frames // LANES
    compute([slot(0, 0)], 0, steps, first=True)
    relay_z(1)
    squares(0, tiles // 2)
    relay_x(0)
    relay_y(1, 0)
    squares(tiles // 2, tiles)
    relay_z(2)
    relay_x(1)
    for r in range(n_z):
        pairs = [(r, s) for s in range(1, n_x)] + ([(r + 1, 0)] if r + 1 < n_z else [])
        for pair in pairs:
            c_copy(*pair, True).wait_recv()
        chunks = [slot(*pair) for pair in pairs]
        last = r + 1 == n_z
        compute(chunks, 0, steps // 2, last=last)
        relay_z(r + 3)
        relay_x(r + 2)
        compute(chunks, steps // 2, steps, last=last)
        relay_y(r + 2, 0)
        for s in range(1, n_x):
            relay_y(r + 1, s)

    pick = (route_ref[...] == lax.broadcasted_iota(jnp.int32, (devices, devices), 0)).astype(jnp.float32)
    sent[...] = jnp.dot(pick, res[...], preferred_element_type=jnp.float32,
                        precision=lax.Precision.HIGHEST).reshape(sent.shape)

    def out_copy(j, incoming):
        dst = lax.rem(me + j, devices)
        src = lax.rem(me + devices - j, devices)
        return pltpu.make_async_remote_copy(
            src_ref=sent.at[dst], dst_ref=got.at[src if incoming else me],
            send_sem=a_send.at[j], recv_sem=a_recv.at[j],
            device_id=(dst // n_clu, dst % n_clu), device_id_type=pl.DeviceIdType.MESH)

    def send(j, carry):
        out_copy(j, False).start()
        return carry

    lax.fori_loop(1, devices, send, 0)
    got[me] = sent[me]
    for r in range(n_z):
        for s in range(n_x):
            if s:
                x_copy(r, s).wait_send()
            elif r:
                z_copy(r).wait_send()
            if r:
                for t in range(1, n_y):
                    y_copy(r, s, t).wait_send()
            if r or s:
                c_copy(r, s).wait_send()

    def receive(j, carry):
        out_copy(j, True).wait_recv()
        return carry

    lax.fori_loop(1, devices, receive, 0)
    out[...] = got[...].reshape(devices, LANES)

    def sent_off(j, carry):
        out_copy(j, False).wait_send()
        return carry

    lax.fori_loop(1, devices, sent_off, 0)


def per_device(n_utt, n_clu, features, centroids, route):
    frames, width = features.shape
    rows = centroids.shape[0]
    devices = n_utt * n_clu
    n_x = 1
    while n_x * n_x * 4 <= n_clu:
        n_x *= 2
    n_z = n_clu // n_x
    per_block = frames // devices
    tiles = 4
    dma = pltpu.SemaphoreType.DMA
    n_y = n_utt // 2
    cent = centroids.reshape(2, n_y, rows // n_utt, width)
    table = pl.pallas_call(
        functools.partial(kernel, n_utt, n_clu, n_x),
        out_shape=jax.ShapeDtypeStruct((devices, LANES), jnp.float32),
        in_specs=[pl.BlockSpec(memory_space=pl.ANY), pl.BlockSpec(memory_space=pl.ANY),
                  pl.BlockSpec(memory_space=pltpu.VMEM)],
        out_specs=pl.BlockSpec(memory_space=pltpu.VMEM),
        scratch_shapes=[
            pltpu.VMEM((frames, width), features.dtype),
            pltpu.VMEM((n_clu,) + cent.shape, centroids.dtype),
            pltpu.VMEM((frames, LANES), jnp.float32),
            pltpu.VMEM((frames, LANES), jnp.int32),
            pltpu.VMEM((frames // LANES, 1, LANES), jnp.float32),
            pltpu.VMEM((8, n_x * LANES), jnp.float32),
            pltpu.VMEM((devices, LANES), jnp.float32),
            pltpu.VMEM((devices, 1, LANES), jnp.float32),
            pltpu.VMEM((devices, 1, LANES), jnp.float32),
            dma((tiles,)), dma(()),
            dma((n_z,)), dma((n_z,)),
            dma((n_z, n_x)), dma((n_z, n_x)),
            dma((n_z, n_x, n_y)), dma((n_z, n_x, n_y)),
            dma((n_z, n_x)), dma((n_z, n_x)),
            dma((devices,)), dma((devices,)),
        ],
        compiler_params=pltpu.CompilerParams(
            collective_id=0, has_side_effects=True, vmem_limit_bytes=60 * 1024 * 1024),
        name="nearest",
    )(features, cent, route)
    labels, least = table[:, :per_block].astype(jnp.int32), table[:, per_block:2 * per_block]
    return labels.reshape(1, devices, per_block), least.reshape(1, devices, per_block)


def solution(mesh):
    placed = (P(("utt", "clu"), None), P("clu", None), P(("utt", "clu"), None))
    return jax.shard_map(
        functools.partial(per_device, mesh.shape["utt"], mesh.shape["clu"]),
        mesh=mesh,
        in_specs=placed,
        out_specs=(P(("utt", "clu"), None, None), P(("utt", "clu"), None, None)),
        check_vma=False,
    )
```

time: 46.2 us -> 42.4 us (0.918)
  local copies, waits for them, and re-layouts: 2.65 us -> 0 us
  Pallas kernels: 42.6 us -> 40 us
  other arithmetic: 0 us -> 1.47 us
    unnamed x2 -> x0, local copies, waits for them, and re-layouts: 2.65 us -> none
    pallas_call x1, Pallas kernels: 42.6 us -> 40 us  [per_device(): pl.pallas_call(functools.partial(kernel, n_utt, n_clu, n_x), out_shape=ja...]
    reshape x0 -> x1, other arithmetic: none -> 1.47 us  [per_device(): least.reshape(1, devices, per_block)]
where the time goes in v2:
time: 42.4 us; the launch traced here: 42.1 us
  Pallas kernels  40 us (94%)
  other arithmetic  1.47 us (3%)
  between operations  0.64 us (2%)
    pallas_call x1, Pallas kernels, per_device(): pl.pallas_call(functools.partial(kernel, n_utt, n_clu, n_x), out_shape=ja...  40 us
    reshape x1, other arithmetic, per_device(): least.reshape(1, devices, per_block)  1.47 us

profile of v2, /device:TPU:0, one launch (start us, length us, event | category | flops | bytes accessed | tf_op | source)
XLA Modules:
  0.0 42.1 jit_solution(4408987864087754321)
XLA Ops:
  0.6 40.0 %nearest.1 = f32[32,128]{1,0:T(8,128)} custom-call(bf16[2048,1280]{1,0:T(8,128)(2,1)} %feat_hbm.1, bf16[2,2,32,1280]{3,2,1,0:T(8,128)(2,1)} %bitcast.5, s32[1,32]{1,0:T(1,128)} %route_ref.1), custom_call_target="tpu_custom_call" | custom-call | tf_op jit(solution)/shard_map/nearest/pallas_call | solution.py:250
  40.6 1.5 %slice_bitcast_fusion = (f32[1,32,64]{2,1,0:T(8,128)}, s32[1,32,64]{2,1,0:T(8,128)}) fusion(f32[32,128]{1,0:T(8,128)} %nearest.1), kind=kLoop, calls=%fused_computation | loop fusion | flops 2048 | bytes 32768 | tf_op jit(solution)/shard_map/reshape | solution.py:278

commit v3 on v2

--- a/solution.py
+++ b/solution.py
@@ -21,7 +21,7 @@
 
 def kernel(n_utt, n_clu, n_x, feat_hbm, cent_hbm, route_ref, out,
            feat, cent, val, idx, fsq, csq, res, sent, got,
-           feat_sem, own_sem, z_send, z_recv, x_send, x_recv, y_send, y_recv, c_send, c_recv, a_send, a_recv):
+           feat_sem, own_sem, d_send, d_recv, y_send, y_recv, c_send, c_recv, a_send, a_recv):
     n_z = n_clu // n_x
     devices = n_utt * n_clu
     utt, clu = lax.axis_index("utt"), lax.axis_index("clu")
@@ -55,7 +55,7 @@
         feat_copy(t).start()
 
     barrier = pltpu.get_barrier_semaphore()
-    peers = ([(utt, slot(r, 0)) for r in range(1, n_z)] + [(utt, slot(0, s)) for s in range(1, n_x)]
+    peers = ([(utt, slot(r, s)) for r in range(n_z) for s in range(n_x) if r or s]
              + [(xor(utt, 2 * t), clu) for t in range(1, n_y)] + [(partner, clu)])
     for peer in peers:
         pl.semaphore_signal(barrier, inc=1, device_id=peer, device_id_type=pl.DeviceIdType.MESH)
@@ -64,13 +64,19 @@
         return pltpu.make_async_remote_copy(src_ref=piece, dst_ref=piece, send_sem=send, recv_sem=recv,
                                             device_id=(u, w), device_id_type=pl.DeviceIdType.MESH)
 
-    def z_copy(r, incoming=False):
-        piece = cent.at[slot(r, 0) if incoming else clu, half, y]
-        return remote(piece, z_send.at[r], z_recv.at[r], utt, slot(r, 0))
-
-    def x_copy(r, s, incoming=False):
-        piece = cent.at[slot(r, s if incoming else 0), half]
-        return remote(piece.at[y] if r else piece, x_send.at[r, s], x_recv.at[r, s], utt, slot(0, s))
+    odd, even = range(1, n_z, 2), range(2, n_z, 2)
+    cols = range(1, n_x)
+    split = [(r, s) for r in odd for s in cols] + [(r, s) for r in even for s in range(n_x)]
+
+    def d_copy(r, s, incoming=False):
+        relayed = s > 0 and r > 0 and r % 2 == 0
+        if incoming:
+            piece = cent.at[slot(r, s), half]
+        else:
+            piece = cent.at[slot(r, 0) if relayed else clu, half]
+        if (r, s) in split:
+            piece = piece.at[y]
+        return remote(piece, d_send.at[r, s], d_recv.at[r, s], utt, slot(0 if relayed else r, s))
 
     def y_copy(r, s, t, incoming=False):
         piece = cent.at[slot(r, s), half, xor(y, t) if incoming else y]
@@ -82,34 +88,38 @@
 
     own.wait()
     pl.semaphore_wait(barrier, len(peers))
-    for s in range(1, n_x):
-        x_copy(0, s).start()
-    for r in range(1, n_z):
-        z_copy(r).start()
-
-    def relay_z(r):
-        if r < n_z:
-            z_copy(r, True).wait_recv()
-            for s in range(1, n_x):
-                x_copy(r, s).start()
-            for t in range(1, n_y):
-                y_copy(r, 0, t).start()
-
-    def relay_x(r):
-        if r < n_z:
-            for s in range(1, n_x):
-                x_copy(r, s, True).wait_recv()
-                if r:
-                    for t in range(1, n_y):
-                        y_copy(r, s, t).start()
-                else:
-                    c_copy(r, s).start()
-
-    def relay_y(r, s):
-        if 0 < r < n_z:
+    for s in cols:
+        d_copy(0, s).start()
+    for r in even:
+        d_copy(r, 0).start()
+    for r in odd:
+        d_copy(r, 0).start()
+    for r in odd:
+        for s in cols:
+            d_copy(r, s).start()
+
+    def landed(pieces):
+        for r, s in pieces:
+            d_copy(r, s, True).wait_recv()
+            if (r, s) in split:
+                if s == 0:
+                    for j in cols:
+                        d_copy(r, j).start()
+                for t in range(1, n_y):
+                    y_copy(r, s, t).start()
+            else:
+                c_copy(r, s).start()
+
+    def joined(pieces):
+        for r, s in pieces:
             for t in range(1, n_y):
                 y_copy(r, s, t, True).wait_recv()
             c_copy(r, s).start()
+
+    def ready(pieces):
+        for r, s in pieces:
+            c_copy(r, s, True).wait_recv()
+        return [slot(r, s) for r, s in pieces]
 
     def block(w):
         return cent[w].reshape(-1, width)
@@ -169,26 +179,34 @@
         feat_copy(t).wait()
     steps, tiles = frames // step, frames // LANES
     compute([slot(0, 0)], 0, steps, first=True)
-    relay_z(1)
     squares(0, tiles // 2)
-    relay_x(0)
-    relay_y(1, 0)
+    near = [(0, s) for s in cols]
+    sides = [(r, 0) for r in odd]
+    far = [(r, 0) for r in even]
+    first_col = [(1, s) for s in cols]
+    rest_col = [(r, s) for r in odd[1:] for s in cols]
+    far_col = [(r, s) for r in even for s in cols]
+    landed(near)
+    landed(far)
     squares(tiles // 2, tiles)
-    relay_z(2)
-    relay_x(1)
-    for r in range(n_z):
-        pairs = [(r, s) for s in range(1, n_x)] + ([(r + 1, 0)] if r + 1 < n_z else [])
-        for pair in pairs:
-            c_copy(*pair, True).wait_recv()
-        chunks = [slot(*pair) for pair in pairs]
-        last = r + 1 == n_z
-        compute(chunks, 0, steps // 2, last=last)
-        relay_z(r + 3)
-        relay_x(r + 2)
-        compute(chunks, steps // 2, steps, last=last)
-        relay_y(r + 2, 0)
-        for s in range(1, n_x):
-            relay_y(r + 1, s)
+    chunks = ready(near)
+    compute(chunks, 0, steps // 2)
+    landed(first_col)
+    landed(sides)
+    compute(chunks, steps // 2, steps)
+    joined(far)
+    landed(rest_col)
+    landed(far_col)
+    chunks = ready(sides)
+    compute(chunks, 0, steps // 2)
+    joined(first_col)
+    compute(chunks, steps // 2, steps)
+    joined(rest_col)
+    chunks = ready(far + first_col)
+    compute(chunks, 0, steps // 2)
+    joined(far_col)
+    compute(chunks, steps // 2, steps)
+    compute(ready(rest_col + far_col), 0, steps, last=True)
 
     pick = (route_ref[...] == lax.broadcasted_iota(jnp.int32, (devices, devices), 0)).astype(jnp.float32)
     sent[...] = jnp.dot(pick, res[...], preferred_element_type=jnp.float32,
@@ -206,19 +224,16 @@
         out_copy(j, False).start()
         return carry
 
-    lax.fori_loop(1, devices, send, 0)
+    lax.fori_loop(1, devices, send, 0, unroll=True)
     got[me] = sent[me]
     for r in range(n_z):
         for s in range(n_x):
-            if s:
-                x_copy(r, s).wait_send()
-            elif r:
-                z_copy(r).wait_send()
-            if r:
+            if r or s:
+                d_copy(r, s).wait_send()
+                c_copy(r, s).wait_send()
+            if (r, s) in split:
                 for t in range(1, n_y):
                     y_copy(r, s, t).wait_send()
-            if r or s:
-                c_copy(r, s).wait_send()
 
     def receive(j, carry):
         out_copy(j, True).wait_recv()
@@ -259,12 +274,11 @@
             pltpu.VMEM((frames, LANES), jnp.float32),
             pltpu.VMEM((frames, LANES), jnp.int32),
             pltpu.VMEM((frames // LANES, 1, LANES), jnp.float32),
-            pltpu.VMEM((8, n_x * LANES), jnp.float32),
+            pltpu.VMEM((8, n_clu * LANES), jnp.float32),
             pltpu.VMEM((devices, LANES), jnp.float32),
             pltpu.VMEM((devices, 1, LANES), jnp.float32),
             pltpu.VMEM((devices, 1, LANES), jnp.float32),
             dma((tiles,)), dma(()),
-            dma((n_z,)), dma((n_z,)),
             dma((n_z, n_x)), dma((n_z, n_x)),
             dma((n_z, n_x, n_y)), dma((n_z, n_x, n_y)),
             dma((n_z, n_x)), dma((n_z, n_x)),

time: 42.4 us -> 40.2 us (0.948)
  Pallas kernels: 40 us -> 37.8 us
    pallas_call x1, Pallas kernels: 40 us -> 37.8 us  [per_device(): pl.pallas_call(functools.partial(kernel, n_utt, n_clu, n_x), out_shape=ja...]
where the time goes in v3:
time: 40.2 us; the launch traced here: 39.9 us
  Pallas kernels  37.8 us (94%)
  other arithmetic  1.47 us (4%)
  between operations  0.64 us (2%)
    pallas_call x1, Pallas kernels, per_device(): pl.pallas_call(functools.partial(kernel, n_utt, n_clu, n_x), out_shape=ja...  37.8 us
    reshape x1, other arithmetic, per_device(): least.reshape(1, devices, per_block)  1.47 us

profile of v3, /device:TPU:0, one launch (start us, length us, event | category | flops | bytes accessed | tf_op | source)
XLA Modules:
  0.0 39.9 jit_solution(14302094895093064192)
XLA Ops:
  0.6 37.8 %nearest.1 = f32[32,128]{1,0:T(8,128)} custom-call(bf16[2048,1280]{1,0:T(8,128)(2,1)} %feat_hbm.1, bf16[2,2,32,1280]{3,2,1,0:T(8,128)(2,1)} %bitcast.5, s32[1,32]{1,0:T(1,128)} %route_ref.1), custom_call_target="tpu_custom_call" | custom-call | tf_op jit(solution)/shard_map/nearest/pallas_call | solution.py:265
  38.5 1.5 %slice_bitcast_fusion = (f32[1,32,64]{2,1,0:T(8,128)}, s32[1,32,64]{2,1,0:T(8,128)}) fusion(f32[32,128]{1,0:T(8,128)} %nearest.1), kind=kLoop, calls=%fused_computation | loop fusion | flops 2048 | bytes 32768 | tf_op jit(solution)/shard_map/reshape | solution.py:292
